TPU v7x, 32 devices: a whole 2x2x4 slice. The times are simulated.
32 devices in a mesh: band: 8 (over z, x), coef: 4 (over y, core).
Axes of the slice: x: 2, y: 2, z: 4, core: 2. Of those that a mesh axis runs over, the one named last changes fastest.
Arguments:
- coeffs: float32 [1024, 262144], P('band', 'coef'), may hold values from -320 to 320
- ref_block: float32 [1024, 262144], P('band', 'coef'), may hold values from -0.01171875 to 0.01171875
- index_map: int32 [262144], P('coef'), may hold values from 0 to 65535, as said below
- band_group: int32 [1024], P('band'), may hold values from 0 to 15
Outputs:
- ortho: float32 [1024, 262144], P('band', 'coef')
- band_residual: float32 [1024], P('band')
- group_residual: float32 [16], replicated
Inputs may be any that keep to these rules, and one draw needn't show every extreme that they name: Within each aligned slab of 65536 coefficients, index_map holds every number of 0 to 65535 once.
All inputs are finite; a program needn't handle non-finite values.
Results may differ from a plain program's by a relative error of at most 0.000098.
Values sent between devices are 32-bit elements; how exact they have to be, the bound alone decides.
A program may use at most 384 MiB of HBM per device.

v0:
```python
import jax
import jax.numpy as jnp
from jax import lax
from jax.sharding import PartitionSpec as P

NB = 1024
NGROUPS = 16


def local(coeffs, ref_block, index_map, band_group):
    columns = lax.all_to_all(coeffs, "band", split_axis=1, concat_axis=0, tiled=True)
    partial_value = jnp.dot(
        columns, columns.T, precision=lax.Precision.HIGHEST, preferred_element_type=jnp.float32
    )
    margin = lax.psum(partial_value, ("band", "coef"))
    factor = jnp.linalg.cholesky(margin)
    ortho_cols = lax.linalg.triangular_solve(factor, columns, left_side=True, lower=True)
    ortho = lax.all_to_all(ortho_cols, "band", split_axis=0, concat_axis=1, tiled=True)
    aligned = jnp.take(ortho, index_map, axis=1)
    squares = jnp.sum((aligned - ref_block) ** 2, axis=1)
    group_range = jnp.arange(NGROUPS, dtype=jnp.int32)
    totals = lax.psum(squares, "coef")
    band_residual = jnp.sqrt(totals + 1e-06)
    onehot = (band_group[:, None] == group_range[None, :]).astype(jnp.float32)
    terms = jnp.dot(
        band_residual, onehot, precision=lax.Precision.HIGHEST, preferred_element_type=jnp.float32
    )
    group_residual = lax.psum(terms, "band") * (NGROUPS / NB)
    return (ortho, band_residual, group_residual)


def solution(mesh):
    return jax.shard_map(
        local,
        mesh=mesh,
        in_specs=(P("band", "coef"), P("band", "coef"), P("coef"), P("band")),
        out_specs=(P("band", "coef"), P("band"), P()),
        check_vma=False,
    )
```

profile of v0, /device:TPU:0, one launch (start us, length us, event | category | flops | bytes accessed | tf_op | source)
XLA Modules:
  0.0 2639.6 jit_solution(11342121475017291769)
XLA Ops:
  7.2 33.4 %copy.17 = f32[128,65536]{0,1:T(8,128)} copy(f32[128,65536]{1,0:T(8,128)} %param.4) | data formatting | bytes 67108864 | tf_op args[0]
  40.6 31.1 %copy.18 = f32[128,8,8192]{2,0,1:T(8,128)} copy(f32[128,8,8192]{0,2,1:T(8,128)} %bitcast.156) | data formatting | bytes 67108864 | tf_op jit(solution)/shard_map/all_to_all | solution.py:11
  71.7 735.1 %all_to_all.38 = f32[128,8,8192]{2,0,1:T(8,128)} all-to-all(f32[128,8,8192]{2,0,1:T(8,128)} %copy.18), channel_id=1, replica_groups=mesh['band'=8,'coef'=4] {'band'}, dimensions={1} | all-to-all | bytes 67108864 | tf_op jit(solution)/shard_map/all_to_all | solution.py:11
  806.8 117.0 %fusion.74 = f32[1024,1024]{0,1:T(8,128)} fusion(f32[1024,8192]{1,0:T(8,128)} %bitcast.157), kind=kOutput, calls=%fused_computation.177 | convolution fusion | flops 103079215104 | bytes 37748736 | tf_op jit(solution)/shard_map/dot_general | solution.py:12
  923.9 141.9 %all-reduce.3.cloned.1.call-done = f32[1024,1024]{0,1:T(8,128)} async-done(((f32[1024,1024]{0,1:T(8,128)}), f32[1024,1024]{0,1:T(8,128)}) %all-reduce.3.cloned.1.call-update) | async-done | bytes 4194320 | tf_op jit(solution)/shard_map/psum | solution.py:15
  1065.7 5.5 copy.20
  1071.2 4.4 fusion.26
  1077.7 11.7 cholesky.223
  1089.5 9.8 custom-call.62
  1099.3 2.5 cholesky.255
  1101.8 2.3 constant_dynamic-update-slice_fusion.32
  1105.7 11.9 cholesky.244
  1118.2 9.8 custom-call.63
  1129.3 2.1 convolution_subtract_fusion.6
  1131.4 11.7 cholesky.468
  1144.4 9.8 custom-call.64
  1155.3 2.3 convolution_subtract_fusion.7
  1157.7 12.1 cholesky.487
  1171.0 9.8 custom-call.65
  1181.9 2.3 convolution_subtract_fusion.8
  1184.3 11.7 cholesky.506
  1197.3 10.0 custom-call.66
  1208.3 2.4 convolution_subtract_fusion.9
  1210.6 11.7 cholesky.526
  1223.6 9.8 custom-call.67
  1234.4 2.0 convolution_subtract_fusion.10
  1236.4 11.9 cholesky.546
  1249.6 9.8 custom-call.68
  1262.1 11.7 cholesky.564
  1280.8 4.8 select_select_fusion
  1285.6 23.2 while.1
  1286.2 2.3 bitcast_dynamic-update-slice_fusion.2
  1289.1 2.3 bitcast_dynamic-update-slice_fusion.2
  1292.0 2.3 bitcast_dynamic-update-slice_fusion.2
  1294.9 2.3 bitcast_dynamic-update-slice_fusion.2
  1297.8 2.3 bitcast_dynamic-update-slice_fusion.2
  1300.7 2.3 bitcast_dynamic-update-slice_fusion.2
  1303.6 2.3 bitcast_dynamic-update-slice_fusion.2
  1306.5 2.2 bitcast_dynamic-update-slice_fusion.2
  1308.8 79.0 %custom-call.69 = f32[8,128,128]{1,2,0:T(8,128)S(1)} custom-call(f32[8,128,128]{2,1,0:T(8,128)S(1)} %get-tuple-element.10), custom_call_target="InvertDiagBlocksLowerTriangular" | custom-call | tf_op jit(solution)/shard_map/triangular_solve | solution.py:17
  1387.8 12.6 constant_dynamic-update-slice_fusion.17
  1400.4 6.9 convolution_subtract_fusion.1
  1407.3 8.2 constant_dynamic-update-slice_fusion.16
  1415.5 7.7 convolution_subtract_fusion
  1423.2 8.4 constant_dynamic-update-slice_fusion.15
  1431.6 12.2 fusion.16
  1443.8 13.9 constant_dynamic-update-slice_fusion.14
  1457.7 14.1 fusion.19
  1471.8 12.5 constant_dynamic-update-slice_fusion.13
  1484.3 17.1 convolution_subtract_fusion.2
  1501.4 6.7 constant_dynamic-update-slice_fusion.12
  1508.2 19.3 convolution_subtract_fusion.4
  1527.5 5.8 constant_dynamic-update-slice_fusion.11
  1533.3 23.5 convolution_subtract_fusion.3
  1556.8 7.9 convolution_dynamic-update-slice_fusion
  1564.7 7.1 all-to-all-start.1
  1571.8 33.4 %copy.22 = f32[128,65536]{0,1:T(8,128)} copy(f32[128,65536]{1,0:T(8,128)} %param.5) | data formatting | bytes 67108864 | tf_op args[1]
  1605.4 687.3 %all-to-all-done.1 = f32[8,128,8192]{2,1,0:T(8,128)} async-done(((f32[8,128,8192]{2,1,0:T(8,128)}), f32[8,128,8192]{2,1,0:T(8,128)}, u32[]{:S(2)}, u32[]{:S(2)}) %all-to-all-start.1) | async-done | bytes 33554464 | tf_op jit(solution)/shard_map/all_to_all | solution.py:18
  2292.7 31.0 %copy.21 = f32[128,8,8192]{0,2,1:T(8,128)} copy(f32[128,8,8192]{2,0,1:T(8,128)} %bitcast.35) | data formatting | bytes 67108864 | tf_op jit(solution)/shard_map/all_to_all | solution.py:18
  2323.7 228.0 %gather_fusion = f32[65536,128]{1,0:T(8,128)} fusion(f32[128,65536]{0,1:T(8,128)} %bitcast.154, s32[65536]{0:T(1024)S(1)} %fusion.45), kind=kCustom, calls=%fused_computation | custom fusion | bytes 67371008 | tf_op jit(solution)/shard_map/jit(_take)/gather | solution.py:19
  2551.7 20.7 fusion.1
  2572.4 5.7 psum.22
  2578.3 33.5 %copy.23 = f32[128,65536]{1,0:T(8,128)} copy(f32[128,65536]{0,1:T(8,128)} %bitcast.155) | data formatting | bytes 67108864
  2611.7 20.3 psum.23
  (70 shorter events, 26.5 us)
Async XLA Ops:
  7.2 1058.6 %all-reduce.3.cloned.1.call-start = ((), (), s32[]{:S(2)}) async-start(), calls=%async_computation.2 | async-start | bytes 8388608 | tf_op jit(solution)/shard_map/psum | solution.py:15
  1075.7 2.0 copy-start.3
  1400.4 31.3 %copy-start = (f32[128,8192]{1,0:T(8,128)}, f32[128,8192]{1,0:T(8,128)S(1)}, u32[]{:S(2)}) copy-start(f32[128,8192]{1,0:T(8,128)S(1)} %get-tuple-element.79) | copy-start | bytes 12582916
  1415.5 16.1 copy-start.1
  1431.6 12.2 copy-start.2
  1564.7 728.0 %all-to-all-start.1 = ((f32[8,128,8192]{2,1,0:T(8,128)}), f32[8,128,8192]{2,1,0:T(8,128)}, u32[]{:S(2)}, u32[]{:S(2)}) async-start(f32[8,128,8192]{2,1,0:T(8,128)} %bitcast.166), calls=%async_computation.1 | async-start | bytes 67108864 | tf_op jit(solution)/shard_map/all_to_all | solution.py:18
  1571.8 33.4 %copy-start.4 = (s32[65536]{0:T(1024)S(1)}, s32[65536]{0:T(1024)}, u32[]{:S(2)}) copy-start(s32[65536]{0:T(1024)} %param.6) | copy-start | bytes 786436
  2551.7 26.4 copy-start.5
  2578.1 33.7 %copy-start.6 = (f32[128]{0:T(128)}, f32[128]{0:T(128)S(1)}, u32[]{:S(2)}) copy-start(f32[128]{0:T(128)S(1)} %add_sqrt_fusion) | copy-start | bytes 1540
Sparse Core Ops, SparseCore 0:
  924.0 141.7 all-reduce.2
where the time goes:
time: 2650 us; the launch traced here: 2640 us
  waiting for transfers between devices  829 us (31%)
  blocking collectives  761 us (29%)
  local copies, waits for them, and re-layouts  424 us (16%)
  matrix products  317 us (12%)
  other arithmetic  282 us (11%)
    all_to_all x1, blocking collectives, local(): lax.all_to_all(coeffs, 'band', split_axis=1, concat_axis=0, tiled=True)  735 us
    all_to_all x1, waiting for transfers between devices, local(): lax.all_to_all(ortho_cols, 'band', split_axis=0, concat_axis=1, tiled=True)  687 us
    gather x1, local copies, waits for them, and re-layouts, local(): aligned = jnp.take(ortho, index_map, axis=1)  228 us
    another operation x15, matrix products, local(): lax.linalg.triangular_solve(factor, columns, left_side=True, lower=True)  177 us
    another operation x30, other arithmetic, local(): factor = jnp.linalg.cholesky(margin)  172 us
    psum x1, waiting for transfers between devices, local(): margin = lax.psum(partial_value, ('band', 'coef'))  142 us
    dot_general x1, matrix products, local(): jnp.dot(columns, columns.T, precision=lax.Precision.HIGHEST, preferred_el...  117 us
    unnamed x17, local copies, waits for them, and re-layouts  102 us
  transfers between devices with their start and end apart: 2, of which 2 were waited for; matrix products, arithmetic and copies ran while one was open for 1% of the time, Pallas kernels for 0%

commit v1 on v0

--- a/solution.py
+++ b/solution.py
@@ -2,6 +2,7 @@
 import jax.numpy as jnp
 from jax import lax
 from jax.sharding import PartitionSpec as P
+from jax.lax import psum
 
 NB = 1024
 NGROUPS = 16
@@ -12,7 +13,13 @@
     partial_value = jnp.dot(
         columns, columns.T, precision=lax.Precision.HIGHEST, preferred_element_type=jnp.float32
     )
-    margin = lax.psum(partial_value, ("band", "coef"))
+
+    def scan_body(raw, which_axis, mesh_ax):
+        for i in (which_axis, mesh_ax):
+            raw = psum(raw, i)
+        return raw
+
+    margin = scan_body(partial_value, "band", "coef")
     factor = jnp.linalg.cholesky(margin)
     ortho_cols = lax.linalg.triangular_solve(factor, columns, left_side=True, lower=True)
     ortho = lax.all_to_all(ortho_cols, "band", split_axis=0, concat_axis=1, tiled=True)

time: 2650 us -> 2750 us (1.038)
  waiting for transfers between devices: 829 us -> 931 us
    psum x1 -> x2, waiting for transfers between devices: 142 us -> 242 us  [scan_body(): raw = psum(raw, i)]
  transfers between devices with their start and end apart: 2 -> 3, of which waited for: 2 -> 3; matrix products, arithmetic and copies ran while one was open for 1% -> 1% of each run, Pallas kernels for 0% -> 0%
where the time goes in v1:
time: 2750 us; the launch traced here: 2740 us
  waiting for transfers between devices  931 us (34%)
  blocking collectives  761 us (28%)
  local copies, waits for them, and re-layouts  424 us (15%)
  matrix products  317 us (12%)
  other arithmetic  282 us (10%)
    all_to_all x1, blocking collectives, local(): lax.all_to_all(coeffs, 'band', split_axis=1, concat_axis=0, tiled=True)  735 us
    all_to_all x1, waiting for transfers between devices, local(): lax.all_to_all(ortho_cols, 'band', split_axis=0, concat_axis=1, tiled=True)  689 us
    psum x2, waiting for transfers between devices, scan_body(): raw = psum(raw, i)  242 us
    gather x1, local copies, waits for them, and re-layouts, local(): aligned = jnp.take(ortho, index_map, axis=1)  228 us
    another operation x15, matrix products, local(): lax.linalg.triangular_solve(factor, columns, left_side=True, lower=True)  177 us
    another operation x30, other arithmetic, local(): factor = jnp.linalg.cholesky(margin)  172 us
    dot_general x1, matrix products, local(): jnp.dot(columns, columns.T, precision=lax.Precision.HIGHEST, preferred_el...  117 us
    unnamed x17, local copies, waits for them, and re-layouts  102 us
  transfers between devices with their start and end apart: 3, of which 3 were waited for; matrix products, arithmetic and copies ran while one was open for 1% of the time, Pallas kernels for 0%

profile of v1, /device:TPU:0, one launch (start us, length us, event | category | flops | bytes accessed | tf_op | source)
XLA Modules:
  0.0 2741.5 jit_solution(10057939582496905601)
XLA Ops:
  7.2 33.4 %copy.17 = f32[128,65536]{0,1:T(8,128)} copy(f32[128,65536]{1,0:T(8,128)} %param.4) | data formatting | bytes 67108864 | tf_op args[0]
  40.6 31.1 %copy.18 = f32[128,8,8192]{2,0,1:T(8,128)} copy(f32[128,8,8192]{0,2,1:T(8,128)} %bitcast.156) | data formatting | bytes 67108864 | tf_op jit(solution)/shard_map/all_to_all | solution.py:12
  71.7 735.1 %all_to_all.38 = f32[128,8,8192]{2,0,1:T(8,128)} all-to-all(f32[128,8,8192]{2,0,1:T(8,128)} %copy.18), channel_id=1, replica_groups=mesh['band'=8,'coef'=4] {'band'}, dimensions={1} | all-to-all | bytes 67108864 | tf_op jit(solution)/shard_map/all_to_all | solution.py:12
  806.8 117.0 %fusion.74 = f32[1024,1024]{0,1:T(8,128)} fusion(f32[1024,8192]{1,0:T(8,128)} %bitcast.157), kind=kOutput, calls=%fused_computation.177 | convolution fusion | flops 103079215104 | bytes 37748736 | tf_op jit(solution)/shard_map/dot_general | solution.py:13
  923.9 155.6 %all-reduce.4.cloned.1.call-done = f32[1024,1024]{0,1:T(8,128)} async-done(((f32[1024,1024]{0,1:T(8,128)}), f32[1024,1024]{0,1:T(8,128)}) %all-reduce.4.cloned.1.call-update) | async-done | bytes 4194320 | tf_op jit(solution)/shard_map/psum | solution.py:19
  1079.6 86.8 %all-reduce.6.cloned.1.call-done = f32[1024,1024]{0,1:T(8,128)} async-done(((f32[1024,1024]{0,1:T(8,128)}), f32[1024,1024]{0,1:T(8,128)}) %all-reduce.6.cloned.1.call-update) | async-done | bytes 4194320 | tf_op jit(solution)/shard_map/psum | solution.py:19
  1166.4 5.5 copy.20
  1171.9 4.4 fusion.26
  1178.4 11.7 cholesky.223
  1190.2 9.8 custom-call.62
  1200.0 2.5 cholesky.255
  1202.5 2.3 constant_dynamic-update-slice_fusion.32
  1206.4 11.9 cholesky.244
  1218.9 9.8 custom-call.63
  1229.9 2.1 convolution_subtract_fusion.6
  1232.1 11.7 cholesky.468
  1245.1 9.8 custom-call.64
  1256.0 2.3 convolution_subtract_fusion.7
  1258.4 12.1 cholesky.487
  1271.7 9.8 custom-call.65
  1282.6 2.3 convolution_subtract_fusion.8
  1285.0 11.7 cholesky.506
  1298.0 10.0 custom-call.66
  1308.9 2.4 convolution_subtract_fusion.9
  1311.3 11.7 cholesky.526
  1324.3 9.8 custom-call.67
  1337.1 11.9 cholesky.546
  1350.3 9.8 custom-call.68
  1362.8 11.7 cholesky.564
  1381.4 4.8 select_select_fusion
  1386.2 23.2 while.1
  1386.8 2.3 bitcast_dynamic-update-slice_fusion.2
  1389.8 2.3 bitcast_dynamic-update-slice_fusion.2
  1392.7 2.3 bitcast_dynamic-update-slice_fusion.2
  1395.6 2.3 bitcast_dynamic-update-slice_fusion.2
  1398.5 2.3 bitcast_dynamic-update-slice_fusion.2
  1401.4 2.3 bitcast_dynamic-update-slice_fusion.2
  1404.3 2.3 bitcast_dynamic-update-slice_fusion.2
  1407.2 2.2 bitcast_dynamic-update-slice_fusion.2
  1409.4 79.0 %custom-call.69 = f32[8,128,128]{1,2,0:T(8,128)S(1)} custom-call(f32[8,128,128]{2,1,0:T(8,128)S(1)} %get-tuple-element.10), custom_call_target="InvertDiagBlocksLowerTriangular" | custom-call | tf_op jit(solution)/shard_map/triangular_solve | solution.py:24
  1488.5 12.6 constant_dynamic-update-slice_fusion.17
  1501.0 6.9 convolution_subtract_fusion.1
  1508.0 8.2 constant_dynamic-update-slice_fusion.16
  1516.2 7.7 convolution_subtract_fusion
  1523.9 8.4 constant_dynamic-update-slice_fusion.15
  1532.3 12.2 fusion.16
  1544.5 13.9 constant_dynamic-update-slice_fusion.14
  1558.4 14.1 fusion.19
  1572.5 12.5 constant_dynamic-update-slice_fusion.13
  1585.0 17.1 convolution_subtract_fusion.2
  1602.1 6.7 constant_dynamic-update-slice_fusion.12
  1608.9 19.3 convolution_subtract_fusion.4
  1628.1 5.8 constant_dynamic-update-slice_fusion.11
  1633.9 23.5 convolution_subtract_fusion.3
  1657.5 7.9 convolution_dynamic-update-slice_fusion
  1665.4 7.1 all-to-all-start.1
  1672.5 33.4 %copy.22 = f32[128,65536]{0,1:T(8,128)} copy(f32[128,65536]{1,0:T(8,128)} %param.5) | data formatting | bytes 67108864 | tf_op args[1]
  1706.1 688.7 %all-to-all-done.1 = f32[8,128,8192]{2,1,0:T(8,128)} async-done(((f32[8,128,8192]{2,1,0:T(8,128)}), f32[8,128,8192]{2,1,0:T(8,128)}, u32[]{:S(2)}, u32[]{:S(2)}) %all-to-all-start.1) | async-done | bytes 33554464 | tf_op jit(solution)/shard_map/all_to_all | solution.py:25
  2394.8 31.0 %copy.21 = f32[128,8,8192]{0,2,1:T(8,128)} copy(f32[128,8,8192]{2,0,1:T(8,128)} %bitcast.35) | data formatting | bytes 67108864 | tf_op jit(solution)/shard_map/all_to_all | solution.py:25
  2425.7 228.0 %gather_fusion = f32[65536,128]{1,0:T(8,128)} fusion(f32[128,65536]{0,1:T(8,128)} %bitcast.154, s32[65536]{0:T(1024)S(1)} %fusion.45), kind=kCustom, calls=%fused_computation | custom fusion | bytes 67371008 | tf_op jit(solution)/shard_map/jit(_take)/gather | solution.py:26
  2653.8 20.7 fusion.1
  2674.5 5.7 psum.30
  2680.3 33.5 %copy.23 = f32[128,65536]{1,0:T(8,128)} copy(f32[128,65536]{0,1:T(8,128)} %bitcast.155) | data formatting | bytes 67108864
  2713.8 20.1 psum.31
  (73 shorter events, 28.6 us)
Async XLA Ops:
  7.2 1072.4 %all-reduce.4.cloned.1.call-start = ((), (), s32[]{:S(2)}) async-start(), calls=%async_computation.2 | async-start | bytes 8388608 | tf_op jit(solution)/shard_map/psum | solution.py:19
  923.8 242.6 %all-reduce.6.cloned.1.call-start = ((), (), s32[]{:S(2)}) async-start(), calls=%async_computation.3 | async-start | bytes 8388608 | tf_op jit(solution)/shard_map/psum | solution.py:19
  1176.4 2.0 copy-start.3
  1501.0 31.3 %copy-start = (f32[128,8192]{1,0:T(8,128)}, f32[128,8192]{1,0:T(8,128)S(1)}, u32[]{:S(2)}) copy-start(f32[128,8192]{1,0:T(8,128)S(1)} %get-tuple-element.79) | copy-start | bytes 12582916
  1516.2 16.1 copy-start.1
  1532.3 12.2 copy-start.2
  1665.4 729.4 %all-to-all-start.1 = ((f32[8,128,8192]{2,1,0:T(8,128)}), f32[8,128,8192]{2,1,0:T(8,128)}, u32[]{:S(2)}, u32[]{:S(2)}) async-start(f32[8,128,8192]{2,1,0:T(8,128)} %bitcast.166), calls=%async_computation.1 | async-start | bytes 67108864 | tf_op jit(solution)/shard_map/all_to_all | solution.py:25
  1672.5 33.4 %copy-start.4 = (s32[65536]{0:T(1024)S(1)}, s32[65536]{0:T(1024)}, u32[]{:S(2)}) copy-start(s32[65536]{0:T(1024)} %param.6) | copy-start | bytes 786436
  2653.8 26.4 copy-start.5
  2680.1 33.7 %copy-start.6 = (f32[128]{0:T(128)}, f32[128]{0:T(128)S(1)}, u32[]{:S(2)}) copy-start(f32[128]{0:T(128)S(1)} %add_sqrt_fusion) | copy-start | bytes 1540
Sparse Core Ops, SparseCore 0:
  924.0 155.5 all-reduce.3
  1081.9 84.4 all-reduce.5
